TPU v7x, 32 devices: a whole 2x2x4 slice. The times are simulated.
32 devices in a mesh: ga: 8 (over z, y), band: 4 (over x, core).
Axes of the slice: x: 2, y: 2, z: 4, core: 2. Of those that a mesh axis runs over, the one named last changes fastest.
Arguments:
- band_coeffs: bfloat16 [8192, 256], P('ga', 'band'), may hold values from -6 to 6
- beta_vectors: bfloat16 [8192, 2048], P('ga'), may hold values from -0.0625 to 0.0625
- atomic_waves: bfloat16 [8192, 1280], P('ga'), may hold values from -0.0625 to 0.0625
- beta_coupling: float32 [2048, 11], replicated, may hold values from -1 to 2
- ortho_inverse: bfloat16 [1280, 1280], replicated, may hold values from -1 to 2
- hubbard_energy: float32 [3], replicated, may hold values from 1 to 4
- band_weight: float32 [256], P('band'), may hold values from 0 to 0.015625
- orbital_start: int32 [1280], replicated, may hold values from 0 to 1277, as said below
- orbital_species: int32 [1280], replicated, may hold values from 0 to 2, as said below
- beta_start: int32 [2048], replicated, may hold values from 0 to 2046, as said below
Outputs:
- hubbard_apply: bfloat16 [8192, 256], P('ga', 'band')
Inputs may be any that keep to these rules, and one draw needn't show every extreme that they name: `orbital_start`: every atom holds 3 or 5 consecutive orbitals; each orbital holds the index of its atom's first orbital. `orbital_species`: orbitals of 5-orbital atoms have species 0 or 1, orbitals of 3-orbital atoms species 2. `beta_start`: every atom holds 2 or 6 consecutive projectors; each projector holds the index of its atom's first projector.
All inputs are finite; a program needn't handle non-finite values.
Results may differ from a plain program's by a relative error of at most 0.0085.
Values sent between devices are 32-bit elements; how exact they have to be, the bound alone decides.
No kernel may reach another device: no remote copies, remote signals or barrier semaphores. Data moves between devices by JAX's collectives and lax.ppermute only.
A program may use at most 64 MiB of HBM per device.

v0:
```python
import jax
import jax.numpy as jnp
from jax import lax
from jax.sharding import PartitionSpec as P

ORB_REACH = 4
BETA_REACH = 5
NSPEC = 3


def rim_shift(extended, reach, offset, rows):
    return lax.slice_in_dim(extended, reach + offset, reach + offset + rows, axis=0)


def same_atom(start_ext, reach, rows):
    centre = rim_shift(start_ext, reach, 0, rows)
    return jnp.stack(
        [
            (rim_shift(start_ext, reach, offset, rows) == centre).astype(jnp.float32)
            for offset in range(-reach, reach + 1)
        ]
    )


def band_apply(coupling, extended, reach, rows):
    total = jnp.zeros((rows, extended.shape[1]), jnp.float32)
    for offset in range(-reach, reach + 1):
        total = total + coupling[offset + reach][:, None] * rim_shift(extended, reach, offset, rows)
    return total


def beta_matrix(beta_coupling, beta_start):
    rows = beta_start.shape[0]
    start_ext = jnp.pad(beta_start, BETA_REACH, constant_values=-1)
    mask = same_atom(start_ext, BETA_REACH, rows)
    padded = jnp.pad(beta_coupling, ((BETA_REACH, BETA_REACH), (0, 0)))
    terms = []
    for offset in range(-BETA_REACH, BETA_REACH + 1):
        mirror = rim_shift(padded, BETA_REACH, offset, rows)[:, BETA_REACH - offset]
        terms.append(0.5 * (beta_coupling[:, BETA_REACH + offset] + mirror))
    return jnp.stack(terms) * mask


def occupancy(extended, weights, mask, reach, rows):
    centre = rim_shift(extended, reach, 0, rows)
    weighted = centre * weights[None, :]
    return (
        jnp.stack(
            [
                jnp.sum(weighted * rim_shift(extended, reach, offset, rows), axis=1)
                for offset in range(-reach, reach + 1)
            ]
        )
        * mask
    )


def hubbard_mix(occupied, u_rows, mask, extended, reach, rows):
    centre_flag = (jnp.arange(2 * reach + 1) == reach).astype(jnp.float32)[:, None]
    potential = u_rows[None, :] * (0.5 * centre_flag - occupied) * mask
    return band_apply(potential, extended, reach, rows)


def per_orbital_u(species, hubbard_energy):
    onehot = (species[:, None] == jnp.arange(NSPEC)[None, :]).astype(jnp.float32)
    return jnp.dot(onehot, hubbard_energy, precision=lax.Precision.HIGHEST)


def shards(
    band_coeffs,
    beta_vectors,
    atomic_waves,
    beta_coupling,
    ortho_inverse,
    hubbard_energy,
    band_weight,
    orbital_start,
    orbital_species,
    beta_start,
):
    highest = lax.Precision.HIGHEST
    nbeta = beta_vectors.shape[1]
    norbit = atomic_waves.shape[1]
    coupling = beta_matrix(beta_coupling, beta_start)
    beta_correlation = lax.psum(
        jnp.dot(beta_vectors.T, band_coeffs, preferred_element_type=jnp.float32), "ga"
    )
    corrected = band_apply(
        coupling, jnp.pad(beta_correlation, ((BETA_REACH, BETA_REACH), (0, 0))), BETA_REACH, nbeta
    ).astype(jnp.bfloat16)
    correlation_psi = (
        band_coeffs.astype(jnp.float32)
        + jnp.dot(beta_vectors, corrected, preferred_element_type=jnp.float32)
    ).astype(jnp.bfloat16)
    partial_value = jnp.dot(atomic_waves.T, correlation_psi, preferred_element_type=jnp.float32)
    u_full = per_orbital_u(orbital_species, hubbard_energy)
    start_full = jnp.pad(orbital_start, ORB_REACH, constant_values=-1)
    ortho_full = ortho_inverse.astype(jnp.float32)
    summed = lax.psum(partial_value, "ga")
    projections = jnp.dot(ortho_full, summed, precision=highest)
    extended = jnp.pad(projections, ((ORB_REACH, ORB_REACH), (0, 0)))
    mask = same_atom(start_full, ORB_REACH, norbit)
    occupied = lax.psum(occupancy(extended, band_weight, mask, ORB_REACH, norbit), "band")
    mixed = hubbard_mix(occupied, u_full, mask, extended, ORB_REACH, norbit)
    rotated = jnp.dot(ortho_full, mixed, precision=highest)
    rotated_half = rotated.astype(jnp.bfloat16)
    hubbard_waves = jnp.dot(atomic_waves, rotated_half, preferred_element_type=jnp.float32)
    wave_half = hubbard_waves.astype(jnp.bfloat16)
    beta_update = lax.psum(
        jnp.dot(beta_vectors.T, wave_half, preferred_element_type=jnp.float32), "ga"
    )
    correction = band_apply(
        coupling, jnp.pad(beta_update, ((BETA_REACH, BETA_REACH), (0, 0))), BETA_REACH, nbeta
    ).astype(jnp.bfloat16)
    return (
        hubbard_waves + jnp.dot(beta_vectors, correction, preferred_element_type=jnp.float32)
    ).astype(jnp.bfloat16)


def solution(mesh):
    placed = (
        P("ga", "band"),
        P("ga", None),
        P("ga", None),
        P(),
        P(),
        P(),
        P("band"),
        P(),
        P(),
        P(),
    )
    return jax.shard_map(
        shards, mesh=mesh, in_specs=placed, out_specs=P("ga", "band"), check_vma=False
    )
```

profile of v0, /device:TPU:0, one launch (start us, length us, event | category | flops | bytes accessed | tf_op | source)
XLA Modules:
  0.0 279.5 jit_solution(14939464274968887758)
XLA Ops:
  6.5 0.0 copy-start
  6.5 0.0 all-reduce.10.cloned.1.call-start
  6.5 4.1 %fusion.134 = f32[2048,64]{0,1:T(8,128)} fusion(bf16[1024,64]{0,1:T(8,128)(2,1)} %param.10, bf16[1024,2048]{1,0:T(8,128)(2,1)} %param.11), kind=kOutput, calls=%fused_computation.207 | convolution fusion | flops 268435456 | bytes 4849664 | tf_op jit(solution)/shard_map/dot_general | solution.py:86
  10.6 0.0 all-reduce.10.cloned.1.call-update
  10.6 0.0 all-reduce.12.cloned.1.call-start
  10.7 0.0 copy-done.3
  10.7 0.1 multiply_bitcast_fusion.8
  10.8 0.9 multiply_bitcast_fusion
  11.6 0.0 copy-done.14
  11.6 0.1 fusion.117
  11.7 0.2 stack.181
  11.9 1.7 stack.160
  13.6 0.1 fusion.132
  13.7 72.5 %all-reduce.10.cloned.1.call-done = f32[2048,64]{0,1:T(8,128)} async-done(((f32[2048,64]{0,1:T(8,128)}), f32[2048,64]{0,1:T(8,128)}) %all-reduce.10.cloned.1.call-update) | async-done | bytes 524304 | tf_op jit(solution)/shard_map/psum | solution.py:85
  86.2 8.8 %convolution_bitcast_fusion.2 = f32[1280,64]{0,1:T(8,128)} fusion(bf16[1024,1280]{1,0:T(8,128)(2,1)} %param.12, bf16[1024,2048]{1,0:T(8,128)(2,1)} %param.11, f32[2048,64]{0,1:T(8,128)} %all-reduce.10.cloned.1.call-done, f32[2048]{0:T(1024)S(1)} %bitcast.85, f32[2048]{0:T(1024)S(1)} %bitcast.87, f32[2048]{0:T(1024)S(1)} %bitcast.89, f32[2048]{0:T(1024)S(1)} %bitcast.91, ...), kind=kOutput, calls=%fused_computation.2 | convolution fusion | flops 439287808 | bytes 7888896 | tf_op jit(solution)/shard_map/dot_general | solution.py:95
  95.0 0.0 copy-done.7
  95.0 0.0 copy-done.8
  95.0 0.0 copy-done.9
  95.1 0.0 copy-done.10
  95.1 0.0 copy-done.11
  95.1 0.0 copy-done.12
  95.1 0.0 copy-done.13
  95.1 0.0 copy-start.15
  95.1 0.0 all-reduce.12.cloned.1.call-update
  95.1 0.0 all-reduce.14.cloned.1.call-start
  95.2 0.0 copy-done.4
  95.2 0.1 fusion.116
  95.4 0.1 stack.208
  95.5 0.0 copy-done.16
  95.5 0.0 copy-done.17
  95.5 0.5 convolution_reduce_fusion
  96.1 69.8 %all-reduce.12.cloned.1.call-done = f32[1280,64]{0,1:T(8,128)} async-done(((f32[1280,64]{0,1:T(8,128)}), f32[1280,64]{0,1:T(8,128)}) %all-reduce.12.cloned.1.call-update) | async-done | bytes 327696 | tf_op jit(solution)/shard_map/psum | solution.py:99
  165.9 4.0 %convolution_bitcast_fusion.1 = f32[1280,64]{0,1:T(8,128)S(1)} fusion(f32[1280,64]{0,1:T(8,128)} %all-reduce.12.cloned.1.call-done, bf16[1280,1280]{1,0:T(8,128)(2,1)S(1)} %copy-done), kind=kOutput, calls=%fused_computation.1 | convolution fusion | flops 1258291200 | bytes 3932160 | tf_op jit(solution)/shard_map/dot_general | solution.py:100
  169.9 0.7 copy-done.2
  170.6 0.0 copy-done.15
  170.6 0.8 fusion.26
  171.5 0.1 stack.191
  171.6 11.1 %psum.30 = f32[9,1280]{1,0:T(8,128)S(1)} all-reduce(f32[9,1280]{1,0:T(8,128)S(1)} %mul.535), channel_id=1, replica_groups=mesh['ga'=8,'band'=4] {'band'}, use_global_device_ids=true, to_apply=%region_11.12 | all-reduce | flops 11520 | bytes 92160 | tf_op jit(solution)/shard_map/psum | solution.py:103
  182.7 0.0 copy-start.1
  182.7 0.1 multiply_multiply_fusion.9
  182.8 0.1 slice_reduce_fusion.8
  183.0 5.8 %convolution_convert_fusion = bf16[64,1280]{1,0:T(8,128)(2,1)S(1)} fusion(bf16[1280,1280]{1,0:T(8,128)(2,1)S(1)} %copy-done, f32[1280,64]{0,1:T(8,128)} %copy-done.2, f32[1280]{0:T(1024)S(1)} %get-tuple-element.15, f32[1280]{0:T(1024)S(1)} %get-tuple-element.16, f32[1280]{0:T(1024)S(1)} %get-tuple-element.17, f32[1280]{0:T(1024)S(1)} %get-tuple-element.18, ...), kind=kOutput, calls=%fused_computation.3 | convolution fusion | flops 1259765760 | bytes 3814400 | tf_op jit(solution)/shard_map/dot_general | solution.py:105
  188.7 2.6 fusion.133
  191.4 0.0 copy-done.1
  191.4 1.7 convolution_bitcast_fusion
  193.1 0.0 all-reduce.14.cloned.1.call-update
  193.1 72.4 %all-reduce.14.cloned.1.call-done = f32[2048,64]{0,1:T(8,128)} async-done(((f32[2048,64]{0,1:T(8,128)}), f32[2048,64]{0,1:T(8,128)}) %all-reduce.14.cloned.1.call-update) | async-done | bytes 524304 | tf_op jit(solution)/shard_map/psum | solution.py:109
  265.5 7.5 %fusion.3 = bf16[1024,64]{0,1:T(8,128)(2,1)} fusion(f32[64,1024]{1,0:T(8,128)S(1)} %fusion.133, bf16[1024,2048]{1,0:T(8,128)(2,1)} %param.11, f32[2048,64]{0,1:T(8,128)} %all-reduce.14.cloned.1.call-done, f32[2048]{0:T(1024)S(1)} %bitcast.86, f32[2048]{0:T(1024)} %bitcast.88, f32[2048]{0:T(1024)} %bitcast.90, f32[2048]{0:T(1024)} %bitcast.92, ...), kind=kOutput, calls=%fused_computation.9 | convolution fusion | flops 271450112 | bytes 5201920 | tf_op jit(solution)/shard_map/dot_general | solution.py:116
  (40 shorter events, 0.2 us)
Async XLA Ops:
  6.5 159.3 %copy-start = (bf16[1280,1280]{1,0:T(8,128)(2,1)S(1)}, bf16[1280,1280]{1,0:T(8,128)(2,1)}, u32[]{:S(2)}) copy-start(bf16[1280,1280]{1,0:T(8,128)(2,1)} %param.14) | copy-start | bytes 9830404
  6.5 4.1 %copy-start.3 = (f32[2048,11]{0,1:T(8,128)S(1)}, f32[2048,11]{0,1:T(8,128)}, u32[]{:S(2)}) copy-start(f32[2048,11]{0,1:T(8,128)} %param.13) | copy-start | bytes 270340
  6.5 5.1 %copy-start.14 = (s32[2048]{0:T(1024)S(1)}, s32[2048]{0:T(1024)}, u32[]{:S(2)}) copy-start(s32[2048]{0:T(1024)} %param.19) | copy-start | bytes 24580
  6.5 79.7 %all-reduce.10.cloned.1.call-start = ((), (), s32[]{:S(2)}) async-start(), calls=%async_computation | async-start | bytes 1048576 | tf_op jit(solution)/shard_map/psum | solution.py:85
  10.6 155.2 %all-reduce.12.cloned.1.call-start = ((), (), s32[]{:S(2)}) async-start(), calls=%async_computation.1 | async-start | bytes 655360 | tf_op jit(solution)/shard_map/psum | solution.py:99
  13.7 81.4 %copy-start.5 = (f32[1,2048]{1,0:T(1,128)}, f32[1,2048]{1,0:T(1,128)S(1)}, u32[]{:S(2)}) copy-start(f32[1,2048]{1,0:T(1,128)S(1)} %get-tuple-element.25) | copy-start | bytes 24580
  13.7 81.4 %copy-start.6 = (f32[1,2048]{1,0:T(1,128)}, f32[1,2048]{1,0:T(1,128)S(1)}, u32[]{:S(2)}) copy-start(f32[1,2048]{1,0:T(1,128)S(1)} %get-tuple-element.26) | copy-start | bytes 24580
  13.7 81.3 %copy-start.7 = (f32[1,2048]{1,0:T(1,128)}, f32[1,2048]{1,0:T(1,128)S(1)}, u32[]{:S(2)}) copy-start(f32[1,2048]{1,0:T(1,128)S(1)} %get-tuple-element.27) | copy-start | bytes 24580
  13.7 81.3 %copy-start.8 = (f32[1,2048]{1,0:T(1,128)}, f32[1,2048]{1,0:T(1,128)S(1)}, u32[]{:S(2)}) copy-start(f32[1,2048]{1,0:T(1,128)S(1)} %get-tuple-element.28) | copy-start | bytes 24580
  13.7 81.3 %copy-start.9 = (f32[1,2048]{1,0:T(1,128)}, f32[1,2048]{1,0:T(1,128)S(1)}, u32[]{:S(2)}) copy-start(f32[1,2048]{1,0:T(1,128)S(1)} %get-tuple-element.29) | copy-start | bytes 24580
  13.7 81.3 %copy-start.10 = (f32[1,2048]{1,0:T(1,128)}, f32[1,2048]{1,0:T(1,128)S(1)}, u32[]{:S(2)}) copy-start(f32[1,2048]{1,0:T(1,128)S(1)} %get-tuple-element.30) | copy-start | bytes 24580
  13.7 81.3 %copy-start.11 = (f32[1,2048]{1,0:T(1,128)}, f32[1,2048]{1,0:T(1,128)S(1)}, u32[]{:S(2)}) copy-start(f32[1,2048]{1,0:T(1,128)S(1)} %get-tuple-element.31) | copy-start | bytes 24580
  13.7 81.3 %copy-start.12 = (f32[1,2048]{1,0:T(1,128)}, f32[1,2048]{1,0:T(1,128)S(1)}, u32[]{:S(2)}) copy-start(f32[1,2048]{1,0:T(1,128)S(1)} %get-tuple-element.32) | copy-start | bytes 24580
  13.7 81.3 %copy-start.13 = (f32[1,2048]{1,0:T(1,128)}, f32[1,2048]{1,0:T(1,128)S(1)}, u32[]{:S(2)}) copy-start(f32[1,2048]{1,0:T(1,128)S(1)} %get-tuple-element.33) | copy-start | bytes 24580
  86.2 8.9 %copy-start.4 = (s32[1280]{0:T(1024)S(1)}, s32[1280]{0:T(1024)}, u32[]{:S(2)}) copy-start(s32[1280]{0:T(1024)} %param.17) | copy-start | bytes 15364
  86.2 9.3 %copy-start.16 = (s32[1280]{0:T(1024)S(1)}, s32[1280]{0:T(1024)}, u32[]{:S(2)}) copy-start(s32[1280]{0:T(1024)} %param.18) | copy-start | bytes 15364
  86.2 9.3 %copy-start.17 = (f32[3]{0:T(128)S(1)}, f32[3]{0:T(128)}, u32[]{:S(2)}) copy-start(f32[3]{0:T(128)} %param.15) | copy-start | bytes 40
  95.1 75.5 %copy-start.15 = (f32[64]{0:T(128)S(1)}, f32[64]{0:T(128)}, u32[]{:S(2)}) copy-start(f32[64]{0:T(128)} %param.16) | copy-start | bytes 772
  95.1 170.4 %all-reduce.14.cloned.1.call-start = ((), (), s32[]{:S(2)}) async-start(), calls=%async_computation.2 | async-start | bytes 1048576 | tf_op jit(solution)/shard_map/psum | solution.py:109
  169.9 0.7 copy-start.2
  182.7 8.7 %copy-start.1 = (bf16[1024,2048]{1,0:T(8,128)(2,1)S(1)}, bf16[1024,2048]{1,0:T(8,128)(2,1)}, u32[]{:S(2)}) copy-start(bf16[1024,2048]{1,0:T(8,128)(2,1)} %param.11) | copy-start | bytes 12582916
Sparse Core Ops, SparseCore 0:
  10.8 75.4 all-reduce.9
  95.2 70.5 all-reduce.11
  193.2 72.2 all-reduce.13
where the time goes:
time: 280 us; the launch traced here: 279 us
  waiting for transfers between devices  215 us (77%)
  matrix products  35 us (12%)
  between operations  13.6 us (5%)
  blocking collectives  11.1 us (4%)
  local copies, waits for them, and re-layouts  3.06 us (1%)
    psum x1, waiting for transfers between devices, shards(): lax.psum(jnp.dot(beta_vectors.T, band_coeffs, preferred_element_type=jnp....  72.5 us
    psum x1, waiting for transfers between devices, shards(): lax.psum(jnp.dot(beta_vectors.T, wave_half, preferred_element_type=jnp.fl...  72.4 us
    psum x1, waiting for transfers between devices, shards(): summed = lax.psum(partial_value, 'ga')  69.8 us
    psum x1, blocking collectives, shards(): lax.psum(occupancy(extended, band_weight, mask, ORB_REACH, norbit), 'band')  11.1 us
    dot_general x1, matrix products, shards(): jnp.dot(atomic_waves.T, correlation_psi, preferred_element_type=jnp.float32)  8.77 us
    dot_general x1, matrix products, shards(): jnp.dot(beta_vectors, correction, preferred_element_type=jnp.float32)  7.46 us
    dot_general x1, matrix products, shards(): rotated = jnp.dot(ortho_full, mixed, precision=highest)  5.79 us
  transfers between devices with their start and end apart: 3, of which 3 were waited for; matrix products, arithmetic and copies ran while one was open for 1% of the time, Pallas kernels for 0%

commit v1 on v0

--- a/solution.py
+++ b/solution.py
@@ -96,7 +96,9 @@
     u_full = per_orbital_u(orbital_species, hubbard_energy)
     start_full = jnp.pad(orbital_start, ORB_REACH, constant_values=-1)
     ortho_full = ortho_inverse.astype(jnp.float32)
-    summed = lax.psum(partial_value, "ga")
+    summed = partial_value
+    for hop in (1, 2, 4):
+        summed = summed + lax.ppermute(summed, "ga", [(dev, dev ^ hop) for dev in range(8)])
     projections = jnp.dot(ortho_full, summed, precision=highest)
     extended = jnp.pad(projections, ((ORB_REACH, ORB_REACH), (0, 0)))
     mask = same_atom(start_full, ORB_REACH, norbit)

time: 280 us -> 240 us (0.86)
  waiting for transfers between devices: 215 us -> 170 us
  starting transfers between devices: 0.09 us -> 3.04 us
    psum x1 -> x0, waiting for transfers between devices: 69.8 us -> none  [shards(): summed = lax.psum(partial_value, 'ga')]
    ppermute x0 -> x3, waiting for transfers between devices: none -> 25.2 us  [shards(): lax.ppermute(summed, 'ga', [(dev, dev ^ hop) for dev in range(8)])]
    ppermute x0 -> x3, starting transfers between devices: none -> 2.99 us  [shards(): lax.ppermute(summed, 'ga', [(dev, dev ^ hop) for dev in range(8)])]
  transfers between devices with their start and end apart: 3 -> 5, of which waited for: 3 -> 5; matrix products, arithmetic and copies ran while one was open for 1% -> 2% of each run, Pallas kernels for 0% -> 0%
where the time goes in v1:
time: 240 us
  waiting for transfers between devices  170 us (71%)
  matrix products  35.1 us (15%)
  between operations  13.8 us (6%)
  blocking collectives  11.1 us (5%)
  other arithmetic  3.75 us (2%)
  local copies, waits for them, and re-layouts  3.06 us (1%)
  starting transfers between devices  3.04 us (1%)
    psum x1, waiting for transfers between devices, shards(): lax.psum(jnp.dot(beta_vectors.T, band_coeffs, preferred_element_type=jnp....  72.5 us
    psum x1, waiting for transfers between devices, shards(): lax.psum(jnp.dot(beta_vectors.T, wave_half, preferred_element_type=jnp.fl...  72.5 us
    ppermute x3, waiting for transfers between devices, shards(): lax.ppermute(summed, 'ga', [(dev, dev ^ hop) for dev in range(8)])  25.2 us
    psum x1, blocking collectives, shards(): lax.psum(occupancy(extended, band_weight, mask, ORB_REACH, norbit), 'band')  11.1 us
    dot_general x1, matrix products, shards(): jnp.dot(atomic_waves.T, correlation_psi, preferred_element_type=jnp.float32)  8.77 us
    dot_general x1, matrix products, shards(): jnp.dot(beta_vectors, correction, preferred_element_type=jnp.float32)  7.46 us
    dot_general x1, matrix products, shards(): rotated = jnp.dot(ortho_full, mixed, precision=highest)  5.79 us
  transfers between devices with their start and end apart: 5, of which 5 were waited for; matrix products, arithmetic and copies ran while one was open for 2% of the time, Pallas kernels for 0%

profile of v1, /device:TPU:0, one launch (start us, length us, event | category | flops | bytes accessed | tf_op | source)
XLA Modules:
  0.0 240.1 jit_solution(16221434971701890934)
XLA Ops:
  6.5 4.1 %fusion.135 = f32[2048,64]{0,1:T(8,128)} fusion(bf16[1024,64]{0,1:T(8,128)(2,1)} %param.10, bf16[1024,2048]{1,0:T(8,128)(2,1)} %param.11), kind=kOutput, calls=%fused_computation.208 | convolution fusion | flops 268435456 | bytes 4849664 | tf_op jit(solution)/shard_map/dot_general | solution.py:86
  10.6 0.0 all-reduce.9.cloned.1.call-update
  10.6 0.0 all-reduce.11.cloned.1.call-start
  10.7 0.0 copy-done.3
  10.7 0.1 multiply_bitcast_fusion.8
  10.8 0.9 multiply_bitcast_fusion
  11.6 0.1 fusion.118
  11.7 0.2 stack.181
  11.9 1.7 stack.160
  13.6 0.1 fusion.133
  13.7 72.5 %all-reduce.9.cloned.1.call-done = f32[2048,64]{0,1:T(8,128)} async-done(((f32[2048,64]{0,1:T(8,128)}), f32[2048,64]{0,1:T(8,128)}) %all-reduce.9.cloned.1.call-update) | async-done | bytes 524304 | tf_op jit(solution)/shard_map/psum | solution.py:85
  86.2 8.8 %convolution_bitcast_fusion.2 = f32[1280,64]{0,1:T(8,128)} fusion(bf16[1024,1280]{1,0:T(8,128)(2,1)} %param.12, bf16[1024,2048]{1,0:T(8,128)(2,1)} %param.11, f32[2048,64]{0,1:T(8,128)} %all-reduce.9.cloned.1.call-done, f32[2048]{0:T(1024)S(1)} %bitcast.84, f32[2048]{0:T(1024)S(1)} %bitcast.86, f32[2048]{0:T(1024)S(1)} %bitcast.88, f32[2048]{0:T(1024)S(1)} %bitcast.90, ...), kind=kOutput, calls=%fused_computation.2 | convolution fusion | flops 439287808 | bytes 7888896 | tf_op jit(solution)/shard_map/dot_general | solution.py:95
  95.0 0.0 copy-done.7
  95.0 0.0 copy-done.8
  95.0 0.0 copy-done.9
  95.1 0.0 copy-done.10
  95.1 0.0 copy-done.11
  95.1 0.0 copy-done.12
  95.1 0.0 copy-done.13
  95.1 0.0 copy-start.15
  95.1 0.8 collective-permute-start
  95.9 7.2 %collective-permute-done = f32[1280,64]{0,1:T(8,128)S(1)} collective-permute-done((f32[1280,64]{0,1:T(8,128)}, f32[1280,64]{0,1:T(8,128)S(1)}, u32[]{:S(2)}, u32[]{:S(2)}) %collective-permute-start) | collective-permute-done | bytes 327712 | tf_op jit(solution)/shard_map/ppermute | solution.py:101
  103.1 1.0 add.261
  104.1 1.3 collective-permute-start.1
  105.4 6.0 %collective-permute-done.1 = f32[1280,64]{0,1:T(8,128)S(1)} collective-permute-done((f32[1280,64]{0,1:T(8,128)S(1)}, f32[1280,64]{0,1:T(8,128)S(1)}, u32[]{:S(2)}, u32[]{:S(2)}) %collective-permute-start.1) | collective-permute-done | bytes 327712 | tf_op jit(solution)/shard_map/ppermute | solution.py:101
  111.4 0.7 add.262
  112.2 0.9 collective-permute-start.2
  113.1 0.0 copy-done.4
  113.1 0.1 fusion.117
  113.3 0.1 stack.208
  113.4 0.0 copy-done.16
  113.4 0.0 copy-done.17
  113.4 0.5 convolution_reduce_fusion
  113.9 12.0 %collective-permute-done.2 = f32[1280,64]{0,1:T(8,128)} collective-permute-done((f32[1280,64]{0,1:T(8,128)}, f32[1280,64]{0,1:T(8,128)}, u32[]{:S(2)}, u32[]{:S(2)}) %collective-permute-start.2) | collective-permute-done | bytes 327712 | tf_op jit(solution)/shard_map/ppermute | solution.py:101
  126.0 4.1 %convolution_bitcast_fusion.1 = f32[1280,64]{0,1:T(8,128)S(1)} fusion(bf16[1280,1280]{1,0:T(8,128)(2,1)S(1)} %copy-done, f32[1280,64]{0,1:T(8,128)} %add.262, f32[1280,64]{0,1:T(8,128)} %collective-permute-done.2), kind=kOutput, calls=%fused_computation.1 | convolution fusion | flops 1258373120 | bytes 4259840 | tf_op jit(solution)/shard_map/dot_general | solution.py:102
  130.1 0.7 copy-done.2
  130.8 0.8 fusion.26
  131.7 0.1 stack.191
  131.9 11.1 %psum.22 = f32[9,1280]{1,0:T(8,128)S(1)} all-reduce(f32[9,1280]{1,0:T(8,128)S(1)} %mul.535), channel_id=1, replica_groups=mesh['ga'=8,'band'=4] {'band'}, use_global_device_ids=true, to_apply=%region_10.11 | all-reduce | flops 11520 | bytes 92160 | tf_op jit(solution)/shard_map/psum | solution.py:105
  142.9 0.0 copy-start.1
  143.0 0.1 multiply_multiply_fusion.9
  143.0 0.1 slice_reduce_fusion.8
  143.2 5.8 %convolution_convert_fusion = bf16[64,1280]{1,0:T(8,128)(2,1)S(1)} fusion(bf16[1280,1280]{1,0:T(8,128)(2,1)S(1)} %copy-done, f32[1280,64]{0,1:T(8,128)} %copy-done.2, f32[1280]{0:T(1024)S(1)} %get-tuple-element.15, f32[1280]{0:T(1024)S(1)} %get-tuple-element.16, f32[1280]{0:T(1024)S(1)} %get-tuple-element.17, f32[1280]{0:T(1024)S(1)} %get-tuple-element.18, ...), kind=kOutput, calls=%fused_computation.3 | convolution fusion | flops 1259765760 | bytes 3814400 | tf_op jit(solution)/shard_map/dot_general | solution.py:107
  149.0 2.6 %fusion.134 = f32[64,1024]{1,0:T(8,128)S(1)} fusion(bf16[64,1280]{1,0:T(8,128)(2,1)S(1)} %convolution_convert_fusion, bf16[1024,1280]{1,0:T(8,128)(2,1)} %param.12), kind=kOutput, calls=%fused_computation.207 | convolution fusion | flops 167772160 | bytes 3047424 | tf_op jit(solution)/shard_map/dot_general | solution.py:109
  151.6 1.7 convolution_bitcast_fusion
  153.3 0.0 all-reduce.11.cloned.1.call-update
  153.3 72.5 %all-reduce.11.cloned.1.call-done = f32[2048,64]{0,1:T(8,128)} async-done(((f32[2048,64]{0,1:T(8,128)}), f32[2048,64]{0,1:T(8,128)}) %all-reduce.11.cloned.1.call-update) | async-done | bytes 524304 | tf_op jit(solution)/shard_map/psum | solution.py:111
  225.8 7.5 %fusion.3 = bf16[1024,64]{0,1:T(8,128)(2,1)} fusion(f32[64,1024]{1,0:T(8,128)S(1)} %fusion.134, bf16[1024,2048]{1,0:T(8,128)(2,1)} %param.11, f32[2048,64]{0,1:T(8,128)} %all-reduce.11.cloned.1.call-done, f32[2048]{0:T(1024)S(1)} %bitcast.85, f32[2048]{0:T(1024)} %bitcast.87, f32[2048]{0:T(1024)} %bitcast.89, f32[2048]{0:T(1024)} %bitcast.91, ...), kind=kOutput, calls=%fused_computation.9 | convolution fusion | flops 271450112 | bytes 5201920 | tf_op jit(solution)/shard_map/dot_general | solution.py:118
  (45 shorter events, 0.2 us)
Async XLA Ops:
  6.5 119.4 %copy-start = (bf16[1280,1280]{1,0:T(8,128)(2,1)S(1)}, bf16[1280,1280]{1,0:T(8,128)(2,1)}, u32[]{:S(2)}) copy-start(bf16[1280,1280]{1,0:T(8,128)(2,1)} %param.14) | copy-start | bytes 9830404
  6.5 4.1 %copy-start.3 = (f32[2048,11]{0,1:T(8,128)S(1)}, f32[2048,11]{0,1:T(8,128)}, u32[]{:S(2)}) copy-start(f32[2048,11]{0,1:T(8,128)} %param.13) | copy-start | bytes 270340
  6.5 5.1 %copy-start.14 = (s32[2048]{0:T(1024)S(1)}, s32[2048]{0:T(1024)}, u32[]{:S(2)}) copy-start(s32[2048]{0:T(1024)} %param.19) | copy-start | bytes 24580
  6.5 79.7 %all-reduce.9.cloned.1.call-start = ((), (), s32[]{:S(2)}) async-start(), calls=%async_computation | async-start | bytes 1048576 | tf_op jit(solution)/shard_map/psum | solution.py:85
  10.6 215.1 %all-reduce.11.cloned.1.call-start = ((), (), s32[]{:S(2)}) async-start(), calls=%async_computation.1 | async-start | bytes 1048576 | tf_op jit(solution)/shard_map/psum | solution.py:111
  13.7 81.4 %copy-start.5 = (f32[1,2048]{1,0:T(1,128)}, f32[1,2048]{1,0:T(1,128)S(1)}, u32[]{:S(2)}) copy-start(f32[1,2048]{1,0:T(1,128)S(1)} %get-tuple-element.25) | copy-start | bytes 24580
  13.7 81.4 %copy-start.6 = (f32[1,2048]{1,0:T(1,128)}, f32[1,2048]{1,0:T(1,128)S(1)}, u32[]{:S(2)}) copy-start(f32[1,2048]{1,0:T(1,128)S(1)} %get-tuple-element.26) | copy-start | bytes 24580
  13.7 81.3 %copy-start.7 = (f32[1,2048]{1,0:T(1,128)}, f32[1,2048]{1,0:T(1,128)S(1)}, u32[]{:S(2)}) copy-start(f32[1,2048]{1,0:T(1,128)S(1)} %get-tuple-element.27) | copy-start | bytes 24580
  13.7 81.3 %copy-start.8 = (f32[1,2048]{1,0:T(1,128)}, f32[1,2048]{1,0:T(1,128)S(1)}, u32[]{:S(2)}) copy-start(f32[1,2048]{1,0:T(1,128)S(1)} %get-tuple-element.28) | copy-start | bytes 24580
  13.7 81.3 %copy-start.9 = (f32[1,2048]{1,0:T(1,128)}, f32[1,2048]{1,0:T(1,128)S(1)}, u32[]{:S(2)}) copy-start(f32[1,2048]{1,0:T(1,128)S(1)} %get-tuple-element.29) | copy-start | bytes 24580
  13.7 81.3 %copy-start.10 = (f32[1,2048]{1,0:T(1,128)}, f32[1,2048]{1,0:T(1,128)S(1)}, u32[]{:S(2)}) copy-start(f32[1,2048]{1,0:T(1,128)S(1)} %get-tuple-element.30) | copy-start | bytes 24580
  13.7 81.3 %copy-start.11 = (f32[1,2048]{1,0:T(1,128)}, f32[1,2048]{1,0:T(1,128)S(1)}, u32[]{:S(2)}) copy-start(f32[1,2048]{1,0:T(1,128)S(1)} %get-tuple-element.31) | copy-start | bytes 24580
  13.7 81.3 %copy-start.12 = (f32[1,2048]{1,0:T(1,128)}, f32[1,2048]{1,0:T(1,128)S(1)}, u32[]{:S(2)}) copy-start(f32[1,2048]{1,0:T(1,128)S(1)} %get-tuple-element.32) | copy-start | bytes 24580
  13.7 81.3 %copy-start.13 = (f32[1,2048]{1,0:T(1,128)}, f32[1,2048]{1,0:T(1,128)S(1)}, u32[]{:S(2)}) copy-start(f32[1,2048]{1,0:T(1,128)S(1)} %get-tuple-element.33) | copy-start | bytes 24580
  86.2 26.8 %copy-start.4 = (s32[1280]{0:T(1024)S(1)}, s32[1280]{0:T(1024)}, u32[]{:S(2)}) copy-start(s32[1280]{0:T(1024)} %param.17) | copy-start | bytes 15364
  86.2 27.1 %copy-start.16 = (s32[1280]{0:T(1024)S(1)}, s32[1280]{0:T(1024)}, u32[]{:S(2)}) copy-start(s32[1280]{0:T(1024)} %param.18) | copy-start | bytes 15364
  86.2 27.2 %copy-start.17 = (f32[3]{0:T(128)S(1)}, f32[3]{0:T(128)}, u32[]{:S(2)}) copy-start(f32[3]{0:T(128)} %param.15) | copy-start | bytes 40
  95.1 35.8 %copy-start.15 = (f32[64]{0:T(128)S(1)}, f32[64]{0:T(128)}, u32[]{:S(2)}) copy-start(f32[64]{0:T(128)} %param.16) | copy-start | bytes 772
  95.1 8.0 %collective-permute-start = (f32[1280,64]{0,1:T(8,128)}, f32[1280,64]{0,1:T(8,128)S(1)}, u32[]{:S(2)}, u32[]{:S(2)}) collective-permute-start(f32[1280,64]{0,1:T(8,128)} %convolution_bitcast_fusion.2), channel_id=1, source_target_pairs={{0,4},{4,0},{8,12},{12,8},{16,20},{20,16},{24,28},{28,24},{1,5},{5... | collective-permute-start | bytes 983048 | tf_op jit(solution)/shard_map/ppermute | solution.py:101
  104.1 7.3 %collective-permute-start.1 = (f32[1280,64]{0,1:T(8,128)S(1)}, f32[1280,64]{0,1:T(8,128)S(1)}, u32[]{:S(2)}, u32[]{:S(2)}) collective-permute-start(f32[1280,64]{0,1:T(8,128)S(1)} %add.261), channel_id=1, source_target_pairs={{0,8},{4,12},{8,0},{12,4},{16,24},{20,28},{24,16},{28,20},{1,9},{5... | collective-permute-start | bytes 983048 | tf_op jit(solution)/shard_map/ppermute | solution.py:101
  112.2 13.8 %collective-permute-start.2 = (f32[1280,64]{0,1:T(8,128)}, f32[1280,64]{0,1:T(8,128)}, u32[]{:S(2)}, u32[]{:S(2)}) collective-permute-start(f32[1280,64]{0,1:T(8,128)} %add.262), channel_id=1, source_target_pairs={{0,16},{4,20},{8,24},{12,28},{16,0},{20,4},{24,8},{28,12},{1,17},{... | collective-permute-start | bytes 983048 | tf_op jit(solution)/shard_map/ppermute | solution.py:101
  130.1 0.7 copy-start.2
  142.9 8.7 %copy-start.1 = (bf16[1024,2048]{1,0:T(8,128)(2,1)S(1)}, bf16[1024,2048]{1,0:T(8,128)(2,1)}, u32[]{:S(2)}) copy-start(bf16[1024,2048]{1,0:T(8,128)(2,1)} %param.11) | copy-start | bytes 12582916
Sparse Core Ops, SparseCore 0:
  10.8 75.4 all-reduce.8
  153.4 72.2 all-reduce.10
